TPU v7x, 32 devices: a whole 2x2x4 slice. The times are simulated.
32 devices in a mesh: groups: 2 (over x), img: 16 (over z, y, core).
Axes of the slice: x: 2, y: 2, z: 4, core: 2. Of those that a mesh axis runs over, the one named last changes fastest.
Arguments:
- tokens: bfloat16 [64, 128, 768], P(('groups', 'img')), parts along dimension 0, may hold values from -6 to 6
- partners: int32 [64, 8], P(('groups', 'img')), parts along dimension 0, may hold values from 0 to 31, as said below
- counts: int32 [64], P(('groups', 'img')), parts along dimension 0, may hold values from 4 to 8, as said below
- gain_query: float32 [768], replicated, may hold values from 0.5 to 12
- gain_memory: float32 [768], replicated, may hold values from 0.25 to 1.75
- w_query: bfloat16 [768, 768], replicated, may hold values from -0.21875 to 0.21875
- w_key: bfloat16 [768, 768], replicated, may hold values from -0.21875 to 0.21875
- w_value: bfloat16 [768, 768], replicated, may hold values from -0.21875 to 0.21875
- w_out: bfloat16 [768, 768], replicated, may hold values from -0.21875 to 0.21875
Outputs:
- mixed: bfloat16 [64, 128, 768], P(('groups', 'img')), parts along dimension 0
There are 2 independent parts, one for each index of `groups`. A program takes and returns all parts, laid end to end along the dimension named above; an argument that names none is the same for every part. Nothing has to cross between parts.
Inputs may be any that keep to these rules, and one draw needn't show every extreme that they name: No image is its own partner. Over the first counts[a] partners of all images a of one device (image i belongs to device i // 2), at most 1 lie with any one device, and every device reaches 1 with some device. `counts`: every device owns an image with 8 pairs.
All inputs are finite; a program needn't handle non-finite values.
Results may differ from a plain program's by a relative error of at most 0.0067.
Values may be sent and summed in bfloat16 or wider, within the bound.
A program may use at most 128 MiB of HBM per device.

v0:
```python
import jax
import jax.numpy as jnp
from jax import lax
from jax.sharding import PartitionSpec as P

HEADS = 12
HEAD_DIM = 64


def normalize(rows, gain):
    rows = rows.astype(jnp.float32)
    center = rows - jnp.mean(rows, axis=-1, keepdims=True)
    spread = jnp.mean(center * center, axis=-1, keepdims=True)
    return center * lax.rsqrt(spread + 1e-06) * gain


def slot_table(partner_rows, count_rows, own_count, peer_count):
    width = partner_rows.shape[1]
    live = (jnp.arange(width, dtype=jnp.int32)[None, :] < count_rows[:, None]).reshape(-1)
    owner = (partner_rows // own_count).reshape(-1)
    onehot = (
        (owner[:, None] == jnp.arange(peer_count, dtype=jnp.int32)[None, :]) & live[:, None]
    ).astype(jnp.int32)
    before = jnp.cumsum(onehot, axis=0) - onehot
    slot = jnp.sum(before * onehot, axis=1)
    return (owner, slot, live)


def shards(tokens, partners, counts, gain_query, gain_memory, w_query, w_key, w_value, w_out):
    own_count, tok_rows, width = tokens.shape
    listed = partners.shape[1]
    peer_count = lax.axis_size("img")
    slot_cap = (own_count * listed + peer_count - 1) // peer_count
    first_image = lax.axis_index("img") * own_count
    rows = tokens.reshape(own_count * tok_rows, width)
    normed_query = normalize(rows, gain_query).astype(jnp.bfloat16)
    normed_memory = normalize(rows, gain_memory).astype(jnp.bfloat16)
    queries = jnp.dot(normed_query, w_query, preferred_element_type=jnp.float32).astype(
        jnp.bfloat16
    )
    queries = queries.reshape(own_count, tok_rows, HEADS, HEAD_DIM)
    my_owner, my_slot, my_live = slot_table(partners, counts, own_count, peer_count)
    target = jnp.where(my_live, my_owner, peer_count)
    request = (
        jnp.full((peer_count, slot_cap), -1, jnp.int32)
        .at[target, my_slot]
        .set(partners.reshape(-1), mode="drop")
    )
    wanted = lax.all_to_all(request, "img", split_axis=0, concat_axis=0, tiled=True)
    used = wanted >= 0
    local_index = jnp.clip(wanted - first_image, 0, own_count - 1)
    pick = jnp.clip(my_owner, 0, peer_count - 1) * slot_cap + jnp.clip(my_slot, 0, slot_cap - 1)
    picked = normed_memory.reshape(own_count, tok_rows, width)[local_index]
    got_memory = lax.all_to_all(
        jnp.where(used[:, :, None, None], picked, jnp.zeros_like(picked)),
        "img",
        split_axis=0,
        concat_axis=0,
        tiled=True,
    )
    pair_memory = got_memory.reshape(peer_count * slot_cap, tok_rows, width)[pick].reshape(
        -1, width
    )
    pair_keys = jnp.dot(pair_memory, w_key, preferred_element_type=jnp.float32).astype(jnp.bfloat16)
    pair_values = jnp.dot(pair_memory, w_value, preferred_element_type=jnp.float32).astype(
        jnp.bfloat16
    )
    pair_keys = pair_keys.reshape(own_count, listed, tok_rows, HEADS, HEAD_DIM)
    pair_values = pair_values.reshape(own_count, listed, tok_rows, HEADS, HEAD_DIM)
    scale = 1.0 / HEAD_DIM**0.5

    def one_image(item):
        query_rows, key_rows, value_rows, count = item
        scores = (
            jnp.einsum("qhd,kjhd->hkqj", query_rows, key_rows, preferred_element_type=jnp.float32)
            * scale
        )
        probs = jax.nn.softmax(scores, axis=-1).astype(jnp.bfloat16)
        pair_context = jnp.einsum(
            "hkqj,kjhd->kqhd", probs, value_rows, preferred_element_type=jnp.float32
        )
        live = jnp.arange(listed, dtype=jnp.int32) < count
        total = jnp.sum(
            jnp.where(live[:, None, None, None], pair_context, jnp.float32(0.0)), axis=0
        )
        return total.reshape(tok_rows, width) / count.astype(jnp.float32)

    context = lax.map(one_image, (queries, pair_keys, pair_values, counts)).astype(jnp.bfloat16)
    mixed = rows.astype(jnp.float32) + jnp.dot(
        context.reshape(-1, width), w_out, preferred_element_type=jnp.float32
    )
    return mixed.astype(jnp.bfloat16).reshape(own_count, tok_rows, width)


def solution(mesh):
    placed = (
        P(("groups", "img"), None, None),
        P(("groups", "img"), None),
        P(("groups", "img")),
        P(),
        P(),
        P(),
        P(),
        P(),
        P(),
    )
    return jax.shard_map(
        shards,
        mesh=mesh,
        in_specs=placed,
        out_specs=P(("groups", "img"), None, None),
        check_vma=False,
    )
```

profile of v0, /device:TPU:13, one launch (start us, length us, event | category | flops | bytes accessed | tf_op | source)
XLA Modules:
  0.0 160.1 jit_solution(5718504146963567102)
XLA Ops:
  0.0 0.0 copy-start
  0.0 0.8 broadcast_clamp_fusion
  0.8 0.1 eq.15
  0.9 0.7 iota_compare_fusion.2
  1.6 0.7 broadcast_select_fusion
  2.3 0.8 reshape.260
  3.1 0.1 lt.81
  3.2 0.1 fusion.22
  3.3 0.2 select_reduce_fusion.1
  3.5 0.1 select_n.74
  3.5 0.1 min.33
  3.6 0.6 scatter_custom_fusion
  4.3 0.7 copy.39
  5.0 6.6 %all-to-all-start = ((s32[16,1,1]{2,1,0:T(1,128)}), s32[16,1,1]{2,1,0:T(1,128)S(1)}, u32[]{:S(2)}, u32[]{:S(2)}) async-start(s32[16,1,1]{2,1,0:T(1,128)} %copy.39), calls=%async_computation | async-start | bytes 16384 | tf_op jit(solution)/shard_map/all_to_all | solution.py:49
  11.5 1.1 convert_reduce_fusion
  12.6 1.2 multiply_reduce_fusion
  13.9 1.2 multiply_convert_fusion
  15.1 0.1 all-to-all-done
  15.2 0.4 fusion.20
  15.6 2.5 %gather_fusion = bf16[16,128,768]{2,1,0:T(8,128)(2,1)} fusion(bf16[2,128,768]{2,1,0:T(8,128)(2,1)S(1)} %multiply_convert_fusion, s32[1024]{0:T(1024)S(1)} %pad_clamp_fusion.1), kind=kCustom, calls=%fused_computation | custom fusion | bytes 6291520 | tf_op jit(solution)/shard_map/gather | solution.py:53
  18.1 0.4 compare_reduce_fusion
  18.5 3.9 %bitcast_select_fusion = bf16[16,1,128,768]{3,2,1,0:T(8,128)(2,1)} fusion(bf16[16,128,768]{2,1,0:T(8,128)(2,1)} %gather_fusion, pred[16]{0:T(512)(128)(4,1)S(1)} %compare_reduce_fusion), kind=kLoop, calls=%fused_computation.28 | loop fusion | flops 1572864 | bytes 6291472 | tf_op jit(solution)/shard_map/jit(_where)/select_n | solution.py:55
  22.3 0.0 copy-start.1
  22.3 0.0 copy-start.5
  22.3 0.0 copy-start.3
  22.3 7.1 %all-to-all-start.1 = ((bf16[16,1,128,768]{3,2,1,0:T(8,128)(2,1)}), bf16[16,1,128,768]{3,2,1,0:T(8,128)(2,1)}, u32[]{:S(2)}, u32[]{:S(2)}) async-start(bf16[16,1,128,768]{3,2,1,0:T(8,128)(2,1)} %bitcast_select_fusion), calls=%async_computation.1 | async-start | bytes 6291456 | tf_op jit(solution)/shard_map/all_to_all | solution.py:54
  29.4 0.0 copy-done.1
  29.4 0.0 copy-done.5
  29.4 0.2 fusion.19
  29.7 0.0 copy-done.3
  29.7 0.5 convolution_convert_fusion.2
  30.2 0.2 copy.42
  30.3 0.1 reshape.234
  30.4 0.1 copy.45
  30.5 68.9 %all-to-all-done.1 = bf16[16,1,128,768]{3,2,1,0:T(8,128)(2,1)} async-done(((bf16[16,1,128,768]{3,2,1,0:T(8,128)(2,1)}), bf16[16,1,128,768]{3,2,1,0:T(8,128)(2,1)}, u32[]{:S(2)}, u32[]{:S(2)}) %all-to-all-start.1) | async-done | bytes 3145760 | tf_op jit(solution)/shard_map/all_to_all | solution.py:54
  99.4 4.3 %gather_fusion.1 = bf16[16,128,768]{2,1,0:T(8,128)(2,1)} fusion(bf16[16,128,768]{2,1,0:T(8,128)(2,1)} %bitcast.14, s32[1024]{0:T(1024)S(1)} %pad_clamp_fusion), kind=kCustom, calls=%fused_computation.1 | custom fusion | bytes 6291520 | tf_op jit(solution)/shard_map/gather | solution.py:61
  103.8 0.0 copy-done
  103.8 6.2 %convolution_convert_fusion.1 = bf16[2048,768]{1,0:T(8,128)(2,1)} fusion(bf16[2048,768]{1,0:T(8,128)(2,1)} %bitcast.100, bf16[768,768]{1,0:T(8,128)(2,1)S(1)} %copy-done), kind=kOutput, calls=%fused_computation.27 | convolution fusion | flops 2417491968 | bytes 7471104 | tf_op jit(solution)/shard_map/dot_general | solution.py:65
  110.0 4.8 %copy.40 = bf16[2048,768]{0,1:T(8,128)(2,1)} copy(bf16[2048,768]{1,0:T(8,128)(2,1)} %convolution_convert_fusion.1) | data formatting | bytes 6291456 | tf_op jit(solution)/shard_map/convert_element_type | solution.py:65
  114.7 0.0 copy-start.2
  114.7 4.7 %copy.56 = bf16[96,8,16,128]{3,2,1,0:T(8,128)(2,1)} copy(bf16[96,8,16,128]{3,1,2,0:T(8,128)(2,1)} %bitcast.97) | data formatting | bytes 6291456
  119.4 0.0 copy-done.2
  119.5 0.0 copy-done.7
  119.5 4.0 %convolution_convert_fusion = bf16[2048,768]{1,0:T(8,128)(2,1)} fusion(bf16[2048,768]{1,0:T(8,128)(2,1)S(1)} %bitcast.101, bf16[768,768]{1,0:T(8,128)(2,1)S(1)} %copy-done.7), kind=kOutput, calls=%fused_computation.26 | convolution fusion | flops 2417491968 | bytes 7471104 | tf_op jit(solution)/shard_map/dot_general | solution.py:64
  123.4 4.8 %copy.41 = bf16[2048,768]{0,1:T(8,128)(2,1)} copy(bf16[2048,768]{1,0:T(8,128)(2,1)} %convolution_convert_fusion) | data formatting | bytes 6291456 | tf_op jit(solution)/shard_map/convert_element_type | solution.py:64
  128.2 4.7 %copy.57 = bf16[96,8,16,128]{3,2,1,0:T(8,128)(2,1)} copy(bf16[96,8,16,128]{3,1,2,0:T(8,128)(2,1)} %bitcast.98) | data formatting | bytes 6291456
  132.8 0.0 copy-done.4
  132.9 0.0 copy-done.6
  132.9 24.7 %while.10 = (s32[]{:T(128)}, bf16[2,128,768]{2,1,0:T(8,128)(2,1)S(1)}, s32[2]{0:T(128)S(1)}, bf16[2,8,128,12,64]{2,1,0,4,3:T(8,128)(2,1)}, bf16[2,8,128,12,64]{2...) while((s32[]{:T(128)}, bf16[2,128,768]{2,1,0:T(8,128)(2,1)S(1)}, s32[2]{0:T(128)S(1)}, ...), condition=%wide.region_9.10_spmd, body=%wide.region_5.9_spmd.sunk | while | flops 413761664 | bytes 36667524 | solution.py:88
  132.9 2.2 %constant_dynamic-slice_fusion.3 = (bf16[1,8,128,12,64]{2,1,0,4,3:T(8,128)(2,1)S(1)}, bf16[1,8,128,12,64]{2,1,0,4,3:T(8,128)(2,1)S(1)}) fusion(bf16[2,8,128,12,64]{2,1,0,4,3:T(8,128)(2,1)} %get-tuple-element.155, s32[]{:T(128)} %get-tuple-element.144, bf16[2,8,128,12,64]{2,1,0,4,3:T(8,128)(2,1)} %get-tuple-element.154), kind=kLoop, calls=%fused_computation.22.clone.1 | loop fusion | bytes 6291460 | tf_op jit(solution)/shard_map/while/body/jit(dynamic_index_in_dim)/dynamic_slice | solution.py:88
  135.0 1.1 fusion.46
  136.1 5.9 %fusion.47 = (f32[12,8,128]{2,1,0:T(8,128)S(1)}, f32[12,8,128,128]{2,3,1,0:T(8,128)S(1)}) fusion(f32[12,8,128,128]{3,2,1,0:T(8,128)S(1)} %fusion.46), kind=kOutput, calls=%fused_computation.70.clone.1 | output fusion | flops 6291583 | bytes 12632064 | tf_op jit(solution)/shard_map/while/body/eval_jaxpr/sub | solution.py:78
  142.0 0.6 dynamic_slice.26
  142.6 0.6 iota_compare_fusion.4
  143.3 1.0 select_reduce_fusion.3
  145.0 0.1 copy.73
  145.2 2.2 %constant_dynamic-slice_fusion.3 = (bf16[1,8,128,12,64]{2,1,0,4,3:T(8,128)(2,1)S(1)}, bf16[1,8,128,12,64]{2,1,0,4,3:T(8,128)(2,1)S(1)}) fusion(bf16[2,8,128,12,64]{2,1,0,4,3:T(8,128)(2,1)} %get-tuple-element.155, s32[]{:T(128)} %get-tuple-element.144, bf16[2,8,128,12,64]{2,1,0,4,3:T(8,128)(2,1)} %get-tuple-element.154), kind=kLoop, calls=%fused_computation.22.clone.1 | loop fusion | bytes 6291460 | tf_op jit(solution)/shard_map/while/body/jit(dynamic_index_in_dim)/dynamic_slice | solution.py:88
  147.4 1.1 fusion.46
  148.5 5.9 %fusion.47 = (f32[12,8,128]{2,1,0:T(8,128)S(1)}, f32[12,8,128,128]{2,3,1,0:T(8,128)S(1)}) fusion(f32[12,8,128,128]{3,2,1,0:T(8,128)S(1)} %fusion.46), kind=kOutput, calls=%fused_computation.70.clone.1 | output fusion | flops 6291583 | bytes 12632064 | tf_op jit(solution)/shard_map/while/body/eval_jaxpr/sub | solution.py:78
  154.4 0.6 dynamic_slice.26
  155.0 0.6 iota_compare_fusion.4
  155.7 1.0 select_reduce_fusion.3
  157.4 0.1 copy.73
  157.6 2.5 %fusion.16 = bf16[256,768]{1,0:T(8,128)(2,1)} fusion(bf16[256,768]{1,0:T(8,128)(2,1)S(1)} %bitcast.102, bf16[768,768]{1,0:T(8,128)(2,1)} %param.19, bf16[256,768]{1,0:T(8,128)(2,1)S(1)} %bitcast.99), kind=kOutput, calls=%fused_computation.30 | convolution fusion | flops 302579712 | bytes 2359296 | tf_op jit(solution)/shard_map/dot_general | solution.py:89
  (14 shorter events, 0.2 us)
Async XLA Ops:
  0.0 103.8 %copy-start = (bf16[768,768]{1,0:T(8,128)(2,1)S(1)}, bf16[768,768]{1,0:T(8,128)(2,1)}, u32[]{:S(2)}) copy-start(bf16[768,768]{1,0:T(8,128)(2,1)} %param.18) | copy-start | bytes 3538948
  5.0 10.3 %all-to-all-start = ((s32[16,1,1]{2,1,0:T(1,128)}), s32[16,1,1]{2,1,0:T(1,128)S(1)}, u32[]{:S(2)}, u32[]{:S(2)}) async-start(s32[16,1,1]{2,1,0:T(1,128)} %copy.39), calls=%async_computation | async-start | bytes 16384 | tf_op jit(solution)/shard_map/all_to_all | solution.py:49
  22.3 7.1 %copy-start.1 = (bf16[2,128,768]{2,1,0:T(8,128)(2,1)S(1)}, bf16[2,128,768]{2,1,0:T(8,128)(2,1)}, u32[]{:S(2)}) copy-start(bf16[2,128,768]{2,1,0:T(8,128)(2,1)} %param.11) | copy-start | bytes 1179652
  22.3 7.1 %copy-start.5 = (f32[768]{0:T(1024)S(1)}, f32[768]{0:T(1024)}, u32[]{:S(2)}) copy-start(f32[768]{0:T(1024)} %param.14) | copy-start | bytes 9220
  22.3 7.3 %copy-start.3 = (bf16[768,768]{1,0:T(8,128)(2,1)S(1)}, bf16[768,768]{1,0:T(8,128)(2,1)}, u32[]{:S(2)}) copy-start(bf16[768,768]{1,0:T(8,128)(2,1)} %param.16) | copy-start | bytes 3538948
  22.3 77.1 %all-to-all-start.1 = ((bf16[16,1,128,768]{3,2,1,0:T(8,128)(2,1)}), bf16[16,1,128,768]{3,2,1,0:T(8,128)(2,1)}, u32[]{:S(2)}, u32[]{:S(2)}) async-start(bf16[16,1,128,768]{3,2,1,0:T(8,128)(2,1)} %bitcast_select_fusion), calls=%async_computation.1 | async-start | bytes 6291456 | tf_op jit(solution)/shard_map/all_to_all | solution.py:54
  114.7 4.7 %copy-start.2 = (bf16[16,128,768]{2,1,0:T(8,128)(2,1)S(1)}, bf16[16,128,768]{2,1,0:T(8,128)(2,1)}, u32[]{:S(2)}) copy-start(bf16[16,128,768]{2,1,0:T(8,128)(2,1)} %gather_fusion.1) | copy-start | bytes 9437188
  114.7 4.7 %copy-start.7 = (bf16[768,768]{1,0:T(8,128)(2,1)S(1)}, bf16[768,768]{1,0:T(8,128)(2,1)}, u32[]{:S(2)}) copy-start(bf16[768,768]{1,0:T(8,128)(2,1)} %param.17) | copy-start | bytes 3538948
  128.2 4.7 %copy-start.4 = (bf16[2,128,768]{2,1,0:T(8,128)(2,1)S(1)}, bf16[2,128,768]{2,1,0:T(8,128)(2,1)}, u32[]{:S(2)}) copy-start(bf16[2,128,768]{2,1,0:T(8,128)(2,1)} %custom-call.4) | copy-start | bytes 1179652
  128.2 4.7 %copy-start.6 = (s32[2]{0:T(128)S(1)}, s32[2]{0:T(128)}, u32[]{:S(2)}) copy-start(s32[2]{0:T(128)} %param.13) | copy-start | bytes 28
where the time goes:
time: 161 us; the launch traced here: 160 us
  waiting for transfers between devices  69 us (43%)
  local copies, waits for them, and re-layouts  34.3 us (21%)
  other arithmetic  24.2 us (15%)
  matrix products  17.3 us (11%)
  starting transfers between devices  13.6 us (8%)
    all_to_all x1, waiting for transfers between devices, shards(): lax.all_to_all(jnp.where(used[:, :, None, None], picked, jnp.zeros_like(p...  68.9 us
    sub x2, other arithmetic, one_image(): probs = jax.nn.softmax(scores, axis=-1).astype(jnp.bfloat16)  11.8 us
    unnamed x18, local copies, waits for them, and re-layouts  9.42 us
    all_to_all x1, starting transfers between devices, shards(): lax.all_to_all(jnp.where(used[:, :, None, None], picked, jnp.zeros_like(p...  7.08 us
    all_to_all x1, starting transfers between devices, shards(): lax.all_to_all(request, 'img', split_axis=0, concat_axis=0, tiled=True)  6.55 us
    dot_general x1, matrix products, shards(): jnp.dot(pair_memory, w_value, preferred_element_type=jnp.float32)  6.18 us
    dynamic_slice x4, local copies, waits for them, and re-layouts, shards(): lax.map(one_image, (queries, pair_keys, pair_values, counts))  5.53 us
    convert_element_type x1, local copies, waits for them, and re-layouts, shards(): jnp.dot(pair_memory, w_value, preferred_element_type=jnp.float32)  4.76 us
  transfers between devices with their start and end apart: 2, of which 2 were waited for; matrix products, arithmetic and copies ran while one was open for 3% of the time, Pallas kernels for 0%

commit v1 on v0

--- a/solution.py
+++ b/solution.py
@@ -5,6 +5,17 @@
 
 HEADS = 12
 HEAD_DIM = 64
+
+
+def split_up(array, dim, devices):
+    before, after = (array.shape[:dim], array.shape[dim + 1 :])
+    return jnp.moveaxis(array.reshape(*before, devices, -1, *after), dim, 0)
+
+
+def in_order(blocks, dim):
+    blocks = jnp.moveaxis(blocks, 0, dim)
+    shape = blocks.shape
+    return blocks.reshape(*shape[:dim], shape[dim] * shape[dim + 1], *shape[dim + 2 :])
 
 
 def normalize(rows, gain):
@@ -51,13 +62,15 @@
     local_index = jnp.clip(wanted - first_image, 0, own_count - 1)
     pick = jnp.clip(my_owner, 0, peer_count - 1) * slot_cap + jnp.clip(my_slot, 0, slot_cap - 1)
     picked = normed_memory.reshape(own_count, tok_rows, width)[local_index]
-    got_memory = lax.all_to_all(
-        jnp.where(used[:, :, None, None], picked, jnp.zeros_like(picked)),
-        "img",
-        split_axis=0,
-        concat_axis=0,
-        tiled=True,
-    )
+    array = jnp.where(used[:, :, None, None], picked, jnp.zeros_like(picked))
+    size, position = (lax.axis_size("img"), lax.axis_index("img"))
+    tiles = split_up(array, 0, size)
+    gathered = [tiles[position]]
+    for step in range(1, size):
+        sent = tiles[(position + step) % size]
+        gathered.append(lax.ppermute(sent, "img", [(i, (i + step) % size) for i in range(size)]))
+    tiles = jnp.stack(gathered)[(position - jnp.arange(size)) % size]
+    got_memory = in_order(tiles, 0)
     pair_memory = got_memory.reshape(peer_count * slot_cap, tok_rows, width)[pick].reshape(
         -1, width
     )

time: 161 us -> 173 us (1.075); the launches traced: 160 us -> 170 us
  waiting for transfers between devices: 69 us -> 50.3 us
  local copies, waits for them, and re-layouts: 34.3 us -> 50.2 us
  starting transfers between devices: 13.6 us -> 20.7 us
  matrix products: 17.3 us -> 22.2 us
    all_to_all x1 -> x0, waiting for transfers between devices: 68.9 us -> none  [shards(): lax.all_to_all(jnp.where(used[:, :, None, None], picked, jnp.zeros_like(p...]
    ppermute x0 -> x15, waiting for transfers between devices: none -> 50.3 us  [shards(): lax.ppermute(sent, 'img', [(i, (i + step) % size) for i in range(size)])]
    ppermute x0 -> x15, starting transfers between devices: none -> 14.2 us  [shards(): lax.ppermute(sent, 'img', [(i, (i + step) % size) for i in range(size)])]
    unnamed x18 -> x33, local copies, waits for them, and re-layouts: 9.42 us -> 18.6 us
    all_to_all x1 -> x0, starting transfers between devices: 7.08 us -> none  [shards(): lax.all_to_all(jnp.where(used[:, :, None, None], picked, jnp.zeros_like(p...]
    gather x0 -> x1, local copies, waits for them, and re-layouts: none -> 4.31 us  [shards(): tiles = jnp.stack(gathered)[(position - jnp.arange(size)) % size]]
    div x2, other arithmetic: 0.09 us -> 2.08 us  [one_image(): return total.reshape(tok_rows, width) / count.astype(jnp.float32)]
    dot_general x2, matrix products: 2.17 us -> 4.02 us  [one_image(): jnp.einsum('qhd,kjhd->hkqj', query_rows, key_rows, preferred_element_type...]
  transfers between devices with their start and end apart: 2 -> 16, of which waited for: 2 -> 10; matrix products, arithmetic and copies ran while one was open for 3% -> 10% of each run, Pallas kernels for 0% -> 0%
where the time goes in v1:
time: 173 us; the launch traced here: 170 us
  waiting for transfers between devices  50.3 us (29%)
  local copies, waits for them, and re-layouts  50.2 us (29%)
  other arithmetic  24.8 us (14%)
  matrix products  22.2 us (13%)
  starting transfers between devices  20.7 us (12%)
    ppermute x15, waiting for transfers between devices, shards(): lax.ppermute(sent, 'img', [(i, (i + step) % size) for i in range(size)])  50.3 us
    unnamed x33, local copies, waits for them, and re-layouts  18.6 us
    ppermute x15, starting transfers between devices, shards(): lax.ppermute(sent, 'img', [(i, (i + step) % size) for i in range(size)])  14.2 us
    sub x2, other arithmetic, one_image(): probs = jax.nn.softmax(scores, axis=-1).astype(jnp.bfloat16)  11.8 us
    all_to_all x1, starting transfers between devices, shards(): lax.all_to_all(request, 'img', split_axis=0, concat_axis=0, tiled=True)  6.55 us
    dot_general x1, matrix products, shards(): jnp.dot(pair_memory, w_value, preferred_element_type=jnp.float32)  6.18 us
    dynamic_slice x4, local copies, waits for them, and re-layouts, shards(): lax.map(one_image, (queries, pair_keys, pair_values, counts))  4.96 us
    convert_element_type x1, local copies, waits for them, and re-layouts, shards(): jnp.dot(pair_memory, w_value, preferred_element_type=jnp.float32)  4.73 us
  transfers between devices with their start and end apart: 16, of which 10 were waited for; matrix products, arithmetic and copies ran while one was open for 10% of the time, Pallas kernels for 0%

profile of v1, /device:TPU:13, one launch (start us, length us, event | category | flops | bytes accessed | tf_op | source)
XLA Modules:
  0.0 169.8 jit_solution(2842850364807580609)
XLA Ops:
  0.0 0.8 broadcast_clamp_fusion
  0.9 0.7 iota_compare_fusion.2
  1.6 0.7 broadcast_select_fusion
  2.3 0.8 reshape.349
  4.9 6.6 %all-to-all-start = ((s32[16,1,1]{2,1,0:T(1,128)}), s32[16,1,1]{2,1,0:T(1,128)S(1)}, u32[]{:S(2)}, u32[]{:S(2)}) async-start(s32[16,1,1]{2,1,0:T(1,128)} %copy.95), calls=%async_computation | async-start | bytes 16384 | tf_op jit(solution)/shard_map/all_to_all | solution.py:60
  11.7 1.1 convert_reduce_fusion
  12.8 1.2 multiply_reduce_fusion
  14.1 1.2 fusion.19
  15.3 1.8 %convolution_convert_fusion.2 = bf16[256,768]{1,0:T(8,128)(2,1)S(1)} fusion(bf16[256,768]{1,0:T(8,128)(2,1)S(1)} %fusion.19, bf16[768,768]{1,0:T(8,128)(2,1)} %param.16), kind=kOutput, calls=%fused_computation.32 | convolution fusion | flops 302186496 | bytes 1966080 | tf_op jit(solution)/shard_map/dot_general | solution.py:49
  17.4 0.8 copy.115
  18.8 2.4 %gather_fusion = bf16[16,128,768]{2,1,0:T(8,128)(2,1)} fusion(bf16[2,128,768]{2,1,0:T(8,128)(2,1)S(1)} %multiply_convert_fusion, s32[1024]{0:T(1024)S(1)} %get-tuple-element.107), kind=kCustom, calls=%fused_computation | custom fusion | bytes 6291520 | tf_op jit(solution)/shard_map/gather | solution.py:64
  21.6 2.3 %fusion.42 = bf16[16,1,128,768]{3,2,1,0:T(8,128)(2,1)S(1)} fusion(bf16[16,128,768]{2,1,0:T(8,128)(2,1)} %gather_fusion, pred[16]{0:T(512)(128)(4,1)S(1)} %compare_reduce_fusion), kind=kLoop, calls=%fused_computation.110 | loop fusion | flops 1572864 | bytes 6291472 | tf_op jit(solution)/shard_map/jit(_where)/select_n | solution.py:65
  25.0 1.5 collective-permute-start
  26.5 1.2 collective-permute-start.1
  28.1 0.8 collective-permute-start.3
  28.9 2.9 %collective-permute-start.4 = (bf16[1,1,128,768]{3,2,1,0:T(8,128)(2,1)S(1)}, bf16[1,1,128,768]{3,2,1,0:T(8,128)(2,1)S(1)}, u32[]{:S(2)}, u32[]{:S(2)}) collective-permute-start(bf16[1,1,128,768]{3,2,1,0:T(8,128)(2,1)S(1)} %get-tuple-element.95), channel_id=1, source_target_pairs={{0,5},{1,6},{2,7},{3,8},{4,9},{5,10},{6,11},{7,12},{8,13},{9,14},{... | collective-permute-start | bytes 589832 | tf_op jit(solution)/shard_map/ppermute | solution.py:71
  31.8 0.7 bitcast_dynamic-update-slice_fusion.15
  32.5 2.1 %collective-permute-start.5 = (bf16[1,1,128,768]{3,2,1,0:T(8,128)(2,1)S(1)}, bf16[1,1,128,768]{3,2,1,0:T(8,128)(2,1)S(1)}, u32[]{:S(2)}, u32[]{:S(2)}) collective-permute-start(bf16[1,1,128,768]{3,2,1,0:T(8,128)(2,1)S(1)} %get-tuple-element.94), channel_id=1, source_target_pairs={{0,6},{1,7},{2,8},{3,9},{4,10},{5,11},{6,12},{7,13},{8,14},{9,15},... | collective-permute-start | bytes 589832 | tf_op jit(solution)/shard_map/ppermute | solution.py:71
  34.6 0.7 bitcast_dynamic-update-slice_fusion.14
  35.3 1.0 collective-permute-done.1
  36.3 0.7 bitcast_dynamic-update-slice_fusion.13
  37.0 2.0 %collective-permute-done.2 = bf16[1,1,128,768]{3,2,1,0:T(8,128)(2,1)S(1)} collective-permute-done((bf16[1,1,128,768]{3,2,1,0:T(8,128)(2,1)S(1)}, bf16[1,1,128,768]{3,2,1,0:T(8,128)(2,1)S(1)}, u32[]{:S(2)}, u32[]{:S(2)}) %collective-permute-start.2) | collective-permute-done | bytes 196640 | tf_op jit(solution)/shard_map/ppermute | solution.py:71
  40.2 4.0 %collective-permute-done.3 = bf16[1,1,128,768]{3,2,1,0:T(8,128)(2,1)S(1)} collective-permute-done((bf16[1,1,128,768]{3,2,1,0:T(8,128)(2,1)S(1)}, bf16[1,1,128,768]{3,2,1,0:T(8,128)(2,1)S(1)}, u32[]{:S(2)}, u32[]{:S(2)}) %collective-permute-start.3) | collective-permute-done | bytes 196640 | tf_op jit(solution)/shard_map/ppermute | solution.py:71
  44.2 0.7 bitcast_dynamic-update-slice_fusion.11
  44.9 27.8 %collective-permute-done.4 = bf16[1,1,128,768]{3,2,1,0:T(8,128)(2,1)S(1)} collective-permute-done((bf16[1,1,128,768]{3,2,1,0:T(8,128)(2,1)S(1)}, bf16[1,1,128,768]{3,2,1,0:T(8,128)(2,1)S(1)}, u32[]{:S(2)}, u32[]{:S(2)}) %collective-permute-start.4) | collective-permute-done | bytes 196640 | tf_op jit(solution)/shard_map/ppermute | solution.py:71
  72.7 0.7 bitcast_dynamic-update-slice_fusion.10
  73.4 3.5 %collective-permute-done.5 = bf16[1,1,128,768]{3,2,1,0:T(8,128)(2,1)S(1)} collective-permute-done((bf16[1,1,128,768]{3,2,1,0:T(8,128)(2,1)S(1)}, bf16[1,1,128,768]{3,2,1,0:T(8,128)(2,1)S(1)}, u32[]{:S(2)}, u32[]{:S(2)}) %collective-permute-start.5) | collective-permute-done | bytes 196640 | tf_op jit(solution)/shard_map/ppermute | solution.py:71
  76.9 2.2 %collective-permute-start.10 = (bf16[1,1,128,768]{3,2,1,0:T(8,128)(2,1)S(1)}, bf16[1,1,128,768]{3,2,1,0:T(8,128)(2,1)S(1)}, u32[]{:S(2)}, u32[]{:S(2)}) collective-permute-start(bf16[1,1,128,768]{3,2,1,0:T(8,128)(2,1)S(1)} %get-tuple-element.89), channel_id=1, source_target_pairs={{0,11},{1,12},{2,13},{3,14},{4,15},{5,0},{6,1},{7,2},{8,3},{9,4},{... | collective-permute-start | bytes 589832 | tf_op jit(solution)/shard_map/ppermute | solution.py:71
  79.1 0.7 bitcast_dynamic-update-slice_fusion.9
  79.8 5.4 %collective-permute-done.6 = bf16[1,1,128,768]{3,2,1,0:T(8,128)(2,1)S(1)} collective-permute-done((bf16[1,1,128,768]{3,2,1,0:T(8,128)(2,1)S(1)}, bf16[1,1,128,768]{3,2,1,0:T(8,128)(2,1)S(1)}, u32[]{:S(2)}, u32[]{:S(2)}) %collective-permute-start.6) | collective-permute-done | bytes 196640 | tf_op jit(solution)/shard_map/ppermute | solution.py:71
  85.9 3.7 %collective-permute-done.7 = bf16[1,1,128,768]{3,2,1,0:T(8,128)(2,1)S(1)} collective-permute-done((bf16[1,1,128,768]{3,2,1,0:T(8,128)(2,1)S(1)}, bf16[1,1,128,768]{3,2,1,0:T(8,128)(2,1)S(1)}, u32[]{:S(2)}, u32[]{:S(2)}) %collective-permute-start.7) | collective-permute-done | bytes 196640 | tf_op jit(solution)/shard_map/ppermute | solution.py:71
  89.5 0.7 bitcast_dynamic-update-slice_fusion.7
  90.2 2.5 %collective-permute-start.13 = (bf16[1,1,128,768]{3,2,1,0:T(8,128)(2,1)S(1)}, bf16[1,1,128,768]{3,2,1,0:T(8,128)(2,1)S(1)}, u32[]{:S(2)}, u32[]{:S(2)}) collective-permute-start(bf16[1,1,128,768]{3,2,1,0:T(8,128)(2,1)S(1)} %get-tuple-element.86), channel_id=1, source_target_pairs={{0,14},{1,15},{2,0},{3,1},{4,2},{5,3},{6,4},{7,5},{8,6},{9,7},{10,... | collective-permute-start | bytes 589832 | tf_op jit(solution)/shard_map/ppermute | solution.py:71
  92.7 0.7 bitcast_dynamic-update-slice_fusion.6
  93.4 0.7 bitcast_dynamic-update-slice_fusion.5
  94.1 0.7 bitcast_dynamic-update-slice_fusion.4
  94.8 0.7 bitcast_dynamic-update-slice_fusion.3
  96.0 0.7 bitcast_dynamic-update-slice_fusion.2
  96.7 0.9 collective-permute-done.13
  97.5 0.7 bitcast_dynamic-update-slice_fusion.1
  98.2 1.7 collective-permute-done.14
  99.9 0.7 bitcast_dynamic-update-slice_fusion
  100.6 4.3 %gather_fusion.1 = bf16[16,128,768]{2,1,0:T(8,128)(2,1)} fusion(bf16[16,128,768]{2,1,0:T(8,128)(2,1)} %bitcast.44, s32[1024]{0:T(1024)S(1)} %pad_clamp_fusion.1), kind=kCustom, calls=%fused_computation.1 | custom fusion | bytes 6291520 | tf_op jit(solution)/shard_map/gather | solution.py:72
  104.9 4.3 %gather_fusion.2 = bf16[16,128,768]{2,1,0:T(8,128)(2,1)} fusion(bf16[16,128,768]{2,1,0:T(8,128)(2,1)} %gather_fusion.1, s32[1024]{0:T(1024)S(1)} %get-tuple-element.106), kind=kCustom, calls=%fused_computation.2 | custom fusion | bytes 6291520 | tf_op jit(solution)/shard_map/gather | solution.py:74
  109.2 6.2 %convolution_convert_fusion.1 = bf16[2048,768]{1,0:T(8,128)(2,1)} fusion(bf16[2048,768]{1,0:T(8,128)(2,1)} %bitcast.151, bf16[768,768]{1,0:T(8,128)(2,1)S(1)} %copy-done), kind=kOutput, calls=%fused_computation.28 | convolution fusion | flops 2417491968 | bytes 7471104 | tf_op jit(solution)/shard_map/dot_general | solution.py:78
  115.3 4.7 %copy.110 = bf16[2048,768]{0,1:T(8,128)(2,1)} copy(bf16[2048,768]{1,0:T(8,128)(2,1)} %convolution_convert_fusion.1) | data formatting | bytes 6291456 | tf_op jit(solution)/shard_map/convert_element_type | solution.py:78
  120.1 3.0 %copy.126 = bf16[96,8,16,128]{3,2,1,0:T(8,128)(2,1)S(1)} copy(bf16[96,8,16,128]{3,1,2,0:T(8,128)(2,1)} %bitcast.148) | data formatting | bytes 6291456
  123.2 3.9 %convolution_convert_fusion = bf16[2048,768]{1,0:T(8,128)(2,1)} fusion(bf16[2048,768]{1,0:T(8,128)(2,1)S(1)} %bitcast.152, bf16[768,768]{1,0:T(8,128)(2,1)S(1)} %copy-done.7), kind=kOutput, calls=%fused_computation.27 | convolution fusion | flops 2417491968 | bytes 7471104 | tf_op jit(solution)/shard_map/dot_general | solution.py:77
  127.2 4.7 %copy.111 = bf16[2048,768]{0,1:T(8,128)(2,1)} copy(bf16[2048,768]{1,0:T(8,128)(2,1)} %convolution_convert_fusion) | data formatting | bytes 6291456 | tf_op jit(solution)/shard_map/convert_element_type | solution.py:77
  131.9 4.6 %copy.127 = bf16[96,8,16,128]{3,2,1,0:T(8,128)(2,1)} copy(bf16[96,8,16,128]{3,1,2,0:T(8,128)(2,1)} %bitcast.149) | data formatting | bytes 6291456
  136.5 30.5 %while.10 = (s32[]{:T(128)}, bf16[2,128,768]{2,1,0:T(8,128)(2,1)}, s32[2]{0:T(128)S(1)}, bf16[2,8,128,12,64]{2,1,0,4,3:T(8,128)(2,1)S(1)}, bf16[2,8,128,12,64]{2...) while((s32[]{:T(128)}, bf16[2,128,768]{2,1,0:T(8,128)(2,1)}, s32[2]{0:T(128)S(1)}, ...), condition=%wide.region_9.10_spmd, body=%wide.region_5.9_spmd.sunk | while | flops 413761664 | bytes 36668540 | solution.py:101
  136.5 1.9 %constant_dynamic-slice_fusion.18 = (bf16[1,8,128,12,64]{2,1,0,4,3:T(8,128)(2,1)S(1)}, bf16[1,8,128,12,64]{2,1,0,4,3:T(8,128)(2,1)S(1)}) fusion(bf16[2,8,128,12,64]{2,1,0,4,3:T(8,128)(2,1)} %get-tuple-element.171, s32[]{:T(128)} %get-tuple-element.160, bf16[2,8,128,12,64]{2,1,0,4,3:T(8,128)(2,1)S(1)} %get-tuple-element.170), kind=kLoop, calls=%fused_computation.23.clone.1 | loop fusion | bytes 6291460 | tf_op jit(solution)/shard_map/while/body/jit(dynamic_index_in_dim)/dynamic_slice | solution.py:101
  138.4 2.0 %fusion.49 = f32[12,8,128,128]{3,2,1,0:T(8,128)S(1)} fusion(bf16[1,8,128,12,64]{2,1,0,4,3:T(8,128)(2,1)S(1)} %get-tuple-element.150, bf16[2,128,12,64]{1,3,2,0:T(8,128)(2,1)} %get-tuple-element.172, s32[]{:T(128)} %get-tuple-element.160), kind=kOutput, calls=%fused_computation.16.clone.1 | convolution fusion | flops 201326592 | bytes 8061440 | tf_op jit(solution)/shard_map/while/body/eval_jaxpr/qhd,kjhd->hkqj/dot_general | solution.py:88
  140.4 5.9 %fusion.50 = (f32[12,8,128]{2,1,0:T(8,128)S(1)}, f32[12,8,128,128]{2,3,1,0:T(8,128)S(1)}) fusion(f32[12,8,128,128]{3,2,1,0:T(8,128)S(1)} %fusion.49), kind=kOutput, calls=%fused_computation.109.clone.1 | output fusion | flops 6291583 | bytes 12632064 | tf_op jit(solution)/shard_map/while/body/eval_jaxpr/sub | solution.py:91
  147.5 1.8 %select_reduce_fusion.3 = f32[12,64,128]{2,1,0:T(8,128)} fusion(bf16[1,8,128,12,64]{2,1,0,4,3:T(8,128)(2,1)S(1)} %get-tuple-element.149, pred[8]{0:T(512)(128)(4,1)S(1)} %iota_compare_fusion.4, f32[12,8,128,128]{2,3,1,0:T(8,128)S(1)} %get-tuple-element.151, f32[12,8,128]{2,1,0:T(8,128)S(1)} %get-tuple-element.152), kind=kOutput, calls=%fused_computation.13.clone.1 | convolution fusion | flops 205946880 | bytes 8306696 | tf_op jit(solution)/shard_map/while/body/eval_jaxpr/hkqj,kjhd->kqhd/dot_general | solution.py:92
  149.8 1.0 broadcast_divide_fusion.2
  151.0 0.7 constant_dynamic-update-slice_fusion.2
  151.7 1.9 %constant_dynamic-slice_fusion.18 = (bf16[1,8,128,12,64]{2,1,0,4,3:T(8,128)(2,1)S(1)}, bf16[1,8,128,12,64]{2,1,0,4,3:T(8,128)(2,1)S(1)}) fusion(bf16[2,8,128,12,64]{2,1,0,4,3:T(8,128)(2,1)} %get-tuple-element.171, s32[]{:T(128)} %get-tuple-element.160, bf16[2,8,128,12,64]{2,1,0,4,3:T(8,128)(2,1)S(1)} %get-tuple-element.170), kind=kLoop, calls=%fused_computation.23.clone.1 | loop fusion | bytes 6291460 | tf_op jit(solution)/shard_map/while/body/jit(dynamic_index_in_dim)/dynamic_slice | solution.py:101
  153.6 2.0 %fusion.49 = f32[12,8,128,128]{3,2,1,0:T(8,128)S(1)} fusion(bf16[1,8,128,12,64]{2,1,0,4,3:T(8,128)(2,1)S(1)} %get-tuple-element.150, bf16[2,128,12,64]{1,3,2,0:T(8,128)(2,1)} %get-tuple-element.172, s32[]{:T(128)} %get-tuple-element.160), kind=kOutput, calls=%fused_computation.16.clone.1 | convolution fusion | flops 201326592 | bytes 8061440 | tf_op jit(solution)/shard_map/while/body/eval_jaxpr/qhd,kjhd->hkqj/dot_general | solution.py:88
  155.6 5.9 %fusion.50 = (f32[12,8,128]{2,1,0:T(8,128)S(1)}, f32[12,8,128,128]{2,3,1,0:T(8,128)S(1)}) fusion(f32[12,8,128,128]{3,2,1,0:T(8,128)S(1)} %fusion.49), kind=kOutput, calls=%fused_computation.109.clone.1 | output fusion | flops 6291583 | bytes 12632064 | tf_op jit(solution)/shard_map/while/body/eval_jaxpr/sub | solution.py:91
  162.7 1.8 %select_reduce_fusion.3 = f32[12,64,128]{2,1,0:T(8,128)} fusion(bf16[1,8,128,12,64]{2,1,0,4,3:T(8,128)(2,1)S(1)} %get-tuple-element.149, pred[8]{0:T(512)(128)(4,1)S(1)} %iota_compare_fusion.4, f32[12,8,128,128]{2,3,1,0:T(8,128)S(1)} %get-tuple-element.151, f32[12,8,128]{2,1,0:T(8,128)S(1)} %get-tuple-element.152), kind=kOutput, calls=%fused_computation.13.clone.1 | convolution fusion | flops 205946880 | bytes 8306696 | tf_op jit(solution)/shard_map/while/body/eval_jaxpr/hkqj,kjhd->kqhd/dot_general | solution.py:92
  165.1 1.0 broadcast_divide_fusion.2
  166.3 0.7 constant_dynamic-update-slice_fusion.2
  167.0 2.8 %fusion.16 = bf16[256,768]{1,0:T(8,128)(2,1)} fusion(bf16[256,768]{1,0:T(8,128)(2,1)} %bitcast.153, bf16[768,768]{1,0:T(8,128)(2,1)} %param.19, bf16[256,768]{1,0:T(8,128)(2,1)} %bitcast.150), kind=kOutput, calls=%fused_computation.31 | convolution fusion | flops 302579712 | bytes 2359296 | tf_op jit(solution)/shard_map/dot_general | solution.py:102
  (63 shorter events, 9.9 us)
Async XLA Ops:
  0.0 109.2 %copy-start = (bf16[768,768]{1,0:T(8,128)(2,1)S(1)}, bf16[768,768]{1,0:T(8,128)(2,1)}, u32[]{:S(2)}) copy-start(bf16[768,768]{1,0:T(8,128)(2,1)} %param.18) | copy-start | bytes 3538948
  4.9 13.5 %all-to-all-start = ((s32[16,1,1]{2,1,0:T(1,128)}), s32[16,1,1]{2,1,0:T(1,128)S(1)}, u32[]{:S(2)}, u32[]{:S(2)}) async-start(s32[16,1,1]{2,1,0:T(1,128)} %copy.95), calls=%async_computation | async-start | bytes 16384 | tf_op jit(solution)/shard_map/all_to_all | solution.py:60
  11.5 6.7 %copy-start.3 = (bf16[2,128,768]{2,1,0:T(8,128)(2,1)S(1)}, bf16[2,128,768]{2,1,0:T(8,128)(2,1)}, u32[]{:S(2)}) copy-start(bf16[2,128,768]{2,1,0:T(8,128)(2,1)} %param.11) | copy-start | bytes 1179652
  11.5 6.7 %copy-start.5 = (f32[768]{0:T(1024)S(1)}, f32[768]{0:T(1024)}, u32[]{:S(2)}) copy-start(f32[768]{0:T(1024)} %param.15) | copy-start | bytes 9220
  21.6 2.8 %copy-start.2 = (bf16[16,128,768]{2,1,0:T(8,128)(2,1)S(1)}, bf16[16,128,768]{2,1,0:T(8,128)(2,1)}, u32[]{:S(2)}) copy-start(bf16[16,128,768]{2,1,0:T(8,128)(2,1)} %gather_fusion) | copy-start | bytes 9437188
  25.0 7.5 %collective-permute-start = (bf16[1,1,128,768]{3,2,1,0:T(8,128)(2,1)S(1)}, bf16[1,1,128,768]{3,2,1,0:T(8,128)(2,1)S(1)}, u32[]{:S(2)}, u32[]{:S(2)}) collective-permute-start(bf16[1,1,128,768]{3,2,1,0:T(8,128)(2,1)S(1)} %get-tuple-element.99), channel_id=1, source_target_pairs={{0,1},{1,2},{2,3},{3,4},{4,5},{5,6},{6,7},{7,8},{8,9},{9,10},{10,1... | collective-permute-start | bytes 589832 | tf_op jit(solution)/shard_map/ppermute | solution.py:71
  26.5 9.8 %collective-permute-start.1 = (bf16[1,1,128,768]{3,2,1,0:T(8,128)(2,1)S(1)}, bf16[1,1,128,768]{3,2,1,0:T(8,128)(2,1)S(1)}, u32[]{:S(2)}, u32[]{:S(2)}) collective-permute-start(bf16[1,1,128,768]{3,2,1,0:T(8,128)(2,1)S(1)} %get-tuple-element.98), channel_id=1, source_target_pairs={{0,2},{1,3},{2,4},{3,5},{4,6},{5,7},{6,8},{7,9},{8,10},{9,11},{10,... | collective-permute-start | bytes 589832 | tf_op jit(solution)/shard_map/ppermute | solution.py:71
  27.7 11.3 %collective-permute-start.2 = (bf16[1,1,128,768]{3,2,1,0:T(8,128)(2,1)S(1)}, bf16[1,1,128,768]{3,2,1,0:T(8,128)(2,1)S(1)}, u32[]{:S(2)}, u32[]{:S(2)}) collective-permute-start(bf16[1,1,128,768]{3,2,1,0:T(8,128)(2,1)S(1)} %get-tuple-element.97), channel_id=1, source_target_pairs={{0,3},{1,4},{2,5},{3,6},{4,7},{5,8},{6,9},{7,10},{8,11},{9,12},{10... | collective-permute-start | bytes 589832 | tf_op jit(solution)/shard_map/ppermute | solution.py:71
  28.1 16.1 %collective-permute-start.3 = (bf16[1,1,128,768]{3,2,1,0:T(8,128)(2,1)S(1)}, bf16[1,1,128,768]{3,2,1,0:T(8,128)(2,1)S(1)}, u32[]{:S(2)}, u32[]{:S(2)}) collective-permute-start(bf16[1,1,128,768]{3,2,1,0:T(8,128)(2,1)S(1)} %get-tuple-element.96), channel_id=1, source_target_pairs={{0,4},{1,5},{2,6},{3,7},{4,8},{5,9},{6,10},{7,11},{8,12},{9,13},{1... | collective-permute-start | bytes 589832 | tf_op jit(solution)/shard_map/ppermute | solution.py:71
  28.9 43.8 %collective-permute-start.4 = (bf16[1,1,128,768]{3,2,1,0:T(8,128)(2,1)S(1)}, bf16[1,1,128,768]{3,2,1,0:T(8,128)(2,1)S(1)}, u32[]{:S(2)}, u32[]{:S(2)}) collective-permute-start(bf16[1,1,128,768]{3,2,1,0:T(8,128)(2,1)S(1)} %get-tuple-element.95), channel_id=1, source_target_pairs={{0,5},{1,6},{2,7},{3,8},{4,9},{5,10},{6,11},{7,12},{8,13},{9,14},{... | collective-permute-start | bytes 589832 | tf_op jit(solution)/shard_map/ppermute | solution.py:71
  32.5 44.4 %collective-permute-start.5 = (bf16[1,1,128,768]{3,2,1,0:T(8,128)(2,1)S(1)}, bf16[1,1,128,768]{3,2,1,0:T(8,128)(2,1)S(1)}, u32[]{:S(2)}, u32[]{:S(2)}) collective-permute-start(bf16[1,1,128,768]{3,2,1,0:T(8,128)(2,1)S(1)} %get-tuple-element.94), channel_id=1, source_target_pairs={{0,6},{1,7},{2,8},{3,9},{4,10},{5,11},{6,12},{7,13},{8,14},{9,15},... | collective-permute-start | bytes 589832 | tf_op jit(solution)/shard_map/ppermute | solution.py:71
  36.3 48.9 %collective-permute-start.6 = (bf16[1,1,128,768]{3,2,1,0:T(8,128)(2,1)S(1)}, bf16[1,1,128,768]{3,2,1,0:T(8,128)(2,1)S(1)}, u32[]{:S(2)}, u32[]{:S(2)}) collective-permute-start(bf16[1,1,128,768]{3,2,1,0:T(8,128)(2,1)S(1)} %get-tuple-element.93), channel_id=1, source_target_pairs={{0,7},{1,8},{2,9},{3,10},{4,11},{5,12},{6,13},{7,14},{8,15},{9,0},... | collective-permute-start | bytes 589832 | tf_op jit(solution)/shard_map/ppermute | solution.py:71
  39.0 50.6 %collective-permute-start.7 = (bf16[1,1,128,768]{3,2,1,0:T(8,128)(2,1)S(1)}, bf16[1,1,128,768]{3,2,1,0:T(8,128)(2,1)S(1)}, u32[]{:S(2)}, u32[]{:S(2)}) collective-permute-start(bf16[1,1,128,768]{3,2,1,0:T(8,128)(2,1)S(1)} %get-tuple-element.92), channel_id=1, source_target_pairs={{0,8},{1,9},{2,10},{3,11},{4,12},{5,13},{6,14},{7,15},{8,0},{9,1},... | collective-permute-start | bytes 589832 | tf_op jit(solution)/shard_map/ppermute | solution.py:71
  44.2 46.0 %collective-permute-start.8 = (bf16[1,1,128,768]{3,2,1,0:T(8,128)(2,1)S(1)}, bf16[1,1,128,768]{3,2,1,0:T(8,128)(2,1)S(1)}, u32[]{:S(2)}, u32[]{:S(2)}) collective-permute-start(bf16[1,1,128,768]{3,2,1,0:T(8,128)(2,1)S(1)} %get-tuple-element.91), channel_id=1, source_target_pairs={{0,9},{1,10},{2,11},{3,12},{4,13},{5,14},{6,15},{7,0},{8,1},{9,2},... | collective-permute-start | bytes 589832 | tf_op jit(solution)/shard_map/ppermute | solution.py:71
  72.7 20.7 %collective-permute-start.9 = (bf16[1,1,128,768]{3,2,1,0:T(8,128)(2,1)S(1)}, bf16[1,1,128,768]{3,2,1,0:T(8,128)(2,1)S(1)}, u32[]{:S(2)}, u32[]{:S(2)}) collective-permute-start(bf16[1,1,128,768]{3,2,1,0:T(8,128)(2,1)S(1)} %get-tuple-element.90), channel_id=1, source_target_pairs={{0,10},{1,11},{2,12},{3,13},{4,14},{5,15},{6,0},{7,1},{8,2},{9,3},... | collective-permute-start | bytes 589832 | tf_op jit(solution)/shard_map/ppermute | solution.py:71
  76.9 17.2 %collective-permute-start.10 = (bf16[1,1,128,768]{3,2,1,0:T(8,128)(2,1)S(1)}, bf16[1,1,128,768]{3,2,1,0:T(8,128)(2,1)S(1)}, u32[]{:S(2)}, u32[]{:S(2)}) collective-permute-start(bf16[1,1,128,768]{3,2,1,0:T(8,128)(2,1)S(1)} %get-tuple-element.89), channel_id=1, source_target_pairs={{0,11},{1,12},{2,13},{3,14},{4,15},{5,0},{6,1},{7,2},{8,3},{9,4},{... | collective-permute-start | bytes 589832 | tf_op jit(solution)/shard_map/ppermute | solution.py:71
  85.2 9.7 %collective-permute-start.11 = (bf16[1,1,128,768]{3,2,1,0:T(8,128)(2,1)S(1)}, bf16[1,1,128,768]{3,2,1,0:T(8,128)(2,1)S(1)}, u32[]{:S(2)}, u32[]{:S(2)}) collective-permute-start(bf16[1,1,128,768]{3,2,1,0:T(8,128)(2,1)S(1)} %get-tuple-element.88), channel_id=1, source_target_pairs={{0,12},{1,13},{2,14},{3,15},{4,0},{5,1},{6,2},{7,3},{8,4},{9,5},{1... | collective-permute-start | bytes 589832 | tf_op jit(solution)/shard_map/ppermute | solution.py:71
  89.5 6.4 %collective-permute-start.12 = (bf16[1,1,128,768]{3,2,1,0:T(8,128)(2,1)S(1)}, bf16[1,1,128,768]{3,2,1,0:T(8,128)(2,1)S(1)}, u32[]{:S(2)}, u32[]{:S(2)}) collective-permute-start(bf16[1,1,128,768]{3,2,1,0:T(8,128)(2,1)S(1)} %get-tuple-element.87), channel_id=1, source_target_pairs={{0,13},{1,14},{2,15},{3,0},{4,1},{5,2},{6,3},{7,4},{8,5},{9,6},{10... | collective-permute-start | bytes 589832 | tf_op jit(solution)/shard_map/ppermute | solution.py:71
  90.2 7.3 %collective-permute-start.13 = (bf16[1,1,128,768]{3,2,1,0:T(8,128)(2,1)S(1)}, bf16[1,1,128,768]{3,2,1,0:T(8,128)(2,1)S(1)}, u32[]{:S(2)}, u32[]{:S(2)}) collective-permute-start(bf16[1,1,128,768]{3,2,1,0:T(8,128)(2,1)S(1)} %get-tuple-element.86), channel_id=1, source_target_pairs={{0,14},{1,15},{2,0},{3,1},{4,2},{5,3},{6,4},{7,5},{8,6},{9,7},{10,... | collective-permute-start | bytes 589832 | tf_op jit(solution)/shard_map/ppermute | solution.py:71
  93.4 6.4 %collective-permute-start.14 = (bf16[1,1,128,768]{3,2,0,1:T(8,128)(2,1)S(1)}, bf16[1,1,128,768]{3,2,0,1:T(8,128)(2,1)S(1)}, u32[]{:S(2)}, u32[]{:S(2)}) collective-permute-start(bf16[1,1,128,768]{3,2,0,1:T(8,128)(2,1)S(1)} %constant_dynamic-slice_fusion.2), channel_id=1, source_target_pairs={{0,15},{1,0},{2,1},{3,2},{4,3},{5,4},{6,5},{7,6},{8,7},{9,8},{10,9... | collective-permute-start | bytes 589832 | tf_op jit(solution)/shard_map/ppermute | solution.py:71
  120.1 3.0 %copy-start.4 = (bf16[16,128,768]{2,1,0:T(8,128)(2,1)S(1)}, bf16[16,128,768]{2,1,0:T(8,128)(2,1)}, u32[]{:S(2)}) copy-start(bf16[16,128,768]{2,1,0:T(8,128)(2,1)} %gather_fusion.2) | copy-start | bytes 9437188
  120.1 3.2 %copy-start.7 = (bf16[768,768]{1,0:T(8,128)(2,1)S(1)}, bf16[768,768]{1,0:T(8,128)(2,1)}, u32[]{:S(2)}) copy-start(bf16[768,768]{1,0:T(8,128)(2,1)} %param.17) | copy-start | bytes 3538948
  131.9 4.6 %copy-start.6 = (s32[2]{0:T(128)S(1)}, s32[2]{0:T(128)}, u32[]{:S(2)}) copy-start(s32[2]{0:T(128)} %param.13) | copy-start | bytes 28
  167.0 2.8 %copy-start.1 = (bf16[768,768]{1,0:T(8,128)(2,1)S(1)}, bf16[768,768]{1,0:T(8,128)(2,1)}, u32[]{:S(2)}) copy-start(bf16[768,768]{1,0:T(8,128)(2,1)} %param.18) | copy-start | bytes 3538948
